TPU v7x, 512 devices: a whole 4x4x16 slice. The times are simulated.
512 devices in a mesh: region: 8 (over z_hi, x), blk: 64 (over y, z_lo, core).
Axes of the slice: x: 4, y: 4, z: 16 (z_hi: 2, z_lo: 8; z = z_hi * 8 + z_lo), core: 2. Of those that a mesh axis runs over, the one named last changes fastest.
Arguments:
- records: float32 [2048, 2048], P(('region', 'blk')), may hold values from -6 to 6
- starts: int32 [2048], P(('region', 'blk')), may hold values from 0 to 1024
- tapers: int32 [2048], P(('region', 'blk')), may hold values from 2 to 256
- pair_a: int32 [393216], P(('region', 'blk')), may hold values from 0 to 3
- pair_b: int32 [393216], P(('region', 'blk')), may hold values from 0 to 255
- pair_count: int32 [512], P(('region', 'blk')), may hold values from 192 to 768, as said below
- observed: float32 [393216, 512], P(('region', 'blk')), may hold values from -6 to 6
Outputs:
- correlations: float32 [393216, 512], P(('region', 'blk'))
- far_correlations: float32 [2048, 512], P(('region', 'blk'))
- adjoint: float32 [2048, 1024], P(('region', 'blk'))
Inputs may be any that keep to these rules, and one draw needn't show every extreme that they name: `pair_count`: device 0 has all 768 slots live.
All inputs are finite; a program needn't handle non-finite values.
Results may differ from a plain program's by a relative error of at most 0.0003.
Values sent between devices are 32-bit elements; how exact they have to be, the bound alone decides.
A program may use at most 64 MiB of HBM per device.

v0:
```python
import math

import jax
import jax.numpy as jnp
from jax import lax
from jax.sharding import PartitionSpec as P

WIN = 1024


def shifted(shard, axis, by):
    size = lax.axis_size(axis)
    return lax.ppermute(shard, axis, [(i, (i + by) % size) for i in range(size)])


def phase_table(rows, cols, length):
    product = rows[:, None] * cols[None, :] % length
    return product.astype(jnp.float32) * (2.0 * math.pi / length)


def taper_windows(records, starts, tapers):
    sample = jnp.arange(WIN, dtype=jnp.int32)
    picked = jnp.take_along_axis(records, starts[:, None] + sample[None, :], axis=1)
    lengths = tapers.astype(jnp.float32)[:, None]
    position = sample.astype(jnp.float32)[None, :]
    shape_fn = jnp.minimum(1.0, jnp.minimum((position + 1.0) / lengths, (WIN - position) / lengths))
    return picked * shape_fn * WIN ** (-0.25)


def to_spectra(windows):
    angle = phase_table(
        jnp.arange(WIN, dtype=jnp.int32), jnp.arange(WIN // 2, dtype=jnp.int32), WIN
    )
    real_part = jnp.dot(windows, jnp.cos(angle), precision=lax.Precision.HIGHEST)
    imag_part = jnp.dot(windows, -jnp.sin(angle), precision=lax.Precision.HIGHEST)
    return jnp.concatenate([real_part, imag_part], axis=1)


def bin_weights():
    bins = jnp.arange(WIN // 2, dtype=jnp.int32)
    weight = jnp.where(bins == 0, 1.0, 2.0).astype(jnp.float32) / WIN
    return jnp.concatenate([weight, weight])


def lag_index():
    return (jnp.arange(WIN // 2, dtype=jnp.int32) - WIN // 4) % WIN


def to_lags(cross_spec):
    angle = phase_table(jnp.arange(WIN // 2, dtype=jnp.int32), lag_index(), WIN)
    table = jnp.concatenate([jnp.cos(angle), -jnp.sin(angle)], axis=0)
    return jnp.dot(cross_spec * bin_weights()[None, :], table, precision=lax.Precision.HIGHEST)


def from_lags(residual):
    angle = phase_table(lag_index(), jnp.arange(WIN // 2, dtype=jnp.int32), WIN)
    table = jnp.concatenate([jnp.cos(angle), -jnp.sin(angle)], axis=1)
    return jnp.dot(residual, table, precision=lax.Precision.HIGHEST)


def to_time(source):
    half = WIN // 2
    angle = phase_table(jnp.arange(half, dtype=jnp.int32), jnp.arange(WIN, dtype=jnp.int32), WIN)
    weighted = source * bin_weights()[None, :]
    first = jnp.dot(weighted[:, :half], jnp.cos(angle), precision=lax.Precision.HIGHEST)
    second = jnp.dot(weighted[:, half:], jnp.sin(angle), precision=lax.Precision.HIGHEST)
    return (first - second) * (1.0 / 16.0)


def cross(left, right):
    half = WIN // 2
    left_r, left_i = (left[:, :half], left[:, half:])
    right_r, right_i = (right[:, :half], right[:, half:])
    return jnp.concatenate(
        [left_r * right_r + left_i * right_i, left_i * right_r - left_r * right_i], axis=1
    )


def times_plain(misfit, spec):
    half = WIN // 2
    mis_r, mis_i = (misfit[:, :half], misfit[:, half:])
    spec_r, spec_i = (spec[:, :half], spec[:, half:])
    return jnp.concatenate(
        [mis_r * spec_r - mis_i * spec_i, mis_r * spec_i + mis_i * spec_r], axis=1
    )


def times_conj(misfit, spec):
    half = WIN // 2
    mis_r, mis_i = (misfit[:, :half], misfit[:, half:])
    spec_r, spec_i = (spec[:, :half], spec[:, half:])
    return jnp.concatenate(
        [mis_r * spec_r + mis_i * spec_i, mis_r * spec_i - mis_i * spec_r], axis=1
    )


def body(records, starts, tapers, pair_a, pair_b, pair_count, observed):
    stations = records.shape[0]
    blocks = lax.axis_size("blk")
    slots = pair_a.shape[0]
    windows = taper_windows(records, starts, tapers)
    spectra = to_spectra(windows)
    group_spec = lax.all_gather(spectra, "blk", axis=0, tiled=True)
    prior = shifted(spectra, "region", 1)
    source_spec = jnp.take(spectra, pair_a, axis=0)
    target_spec = jnp.take(group_spec, pair_b, axis=0)
    live_rows = (jnp.arange(slots, dtype=jnp.int32) < pair_count[0]).astype(jnp.float32)[:, None]
    corr_raw = to_lags(cross(source_spec, target_spec))
    misfit = from_lags((corr_raw - observed) * live_rows)
    group_onehot = (
        jnp.arange(stations * blocks, dtype=jnp.int32)[:, None] == pair_b[None, :]
    ).astype(jnp.float32)
    remote_terms = jnp.dot(
        group_onehot, times_conj(misfit, source_spec), precision=lax.Precision.HIGHEST
    )
    own_onehot = (jnp.arange(stations, dtype=jnp.int32)[:, None] == pair_a[None, :]).astype(
        jnp.float32
    )
    local_terms = jnp.dot(
        own_onehot, times_plain(misfit, target_spec), precision=lax.Precision.HIGHEST
    )
    far_correlations = to_lags(cross(spectra, prior))
    returned = lax.psum_scatter(remote_terms, "blk", scatter_dimension=0, tiled=True)
    adjoint = to_time(local_terms + returned)
    return (corr_raw * live_rows, far_correlations, adjoint)


def solution(mesh):
    in_specs = (
        P(("region", "blk"), None),
        P(("region", "blk")),
        P(("region", "blk")),
        P(("region", "blk")),
        P(("region", "blk")),
        P(("region", "blk")),
        P(("region", "blk"), None),
    )
    out_specs = (P(("region", "blk"), None), P(("region", "blk"), None), P(("region", "blk"), None))
    return jax.shard_map(body, mesh=mesh, in_specs=in_specs, out_specs=out_specs, check_vma=False)
```

profile of v0, /device:TPU:1, one launch (start us, length us, event | category | flops | bytes accessed | tf_op | source)
XLA Modules:
  0.0 1073.0 jit_solution(7538603702445230818)
XLA Ops:
  7.2 0.7 fusion.78
  8.0 34.9 %gather_fusion.2 = f32[4096]{0:T(1024)S(1)} fusion(f32[4,2048]{1,0:T(4,128)S(1)} %copy-done, s32[4096]{0:T(1024)S(1)} %bitcast.13), kind=kCustom, calls=%fused_computation.2 | custom fusion | bytes 65536 | tf_op jit(solution)/shard_map/jit(take_along_axis)/gather | solution.py:23
  43.1 8.9 fusion.27
  52.0 8.7 fusion.30
  62.2 2.5 gather_fusion
  64.9 9.3 fusion.69
  74.2 1.9 broadcast_select_fusion.1
  76.1 111.2 %all-gather.3.cloned.1.call-done = f32[64,4,1024]{2,1,0:T(4,128)} async-done(((f32[1,4,1024]{2,1,0:T(4,128)}), f32[64,4,1024]{2,1,0:T(4,128)}) %all-gather.3.cloned.1.call-update) | async-done | bytes 1048592 | tf_op jit(solution)/shard_map/all_gather | solution.py:103
  187.3 1.6 reshape.148
  188.9 3.6 gather_fusion.1
  192.5 2.3 broadcast_select_fusion
  195.4 0.8 multiply_add_fusion.2
  196.9 6.2 broadcast_multiply_fusion
  203.2 5.3 fusion.17
  208.4 3.1 multiply_add_fusion
  211.5 3.0 fusion.7
  214.6 3.1 collective-permute-start
  217.7 1.3 dynamic-slice
  219.6 10.3 collective-permute-done
  230.0 1.7 fusion.36
  231.7 812.9 %all-reduce.3.cloned.1.call-done = f32[256,1024]{1,0:T(8,128)} async-done(((f32[256,1024]{1,0:T(8,128)}), f32[256,1024]{1,0:T(8,128)}) %all-reduce.3.cloned.1.call-update) | async-done | bytes 1048592
  1044.5 3.0 fusion.49
  1047.5 9.0 fusion.21
  1056.5 9.7 fusion.43
  (43 shorter events, 2.4 us)
Async XLA Ops:
  7.2 0.8 copy-start
  7.2 180.1 %all-gather.3.cloned.1.call-start = ((), (), s32[]{:S(2)}) async-start(), calls=%async_computation | async-start | bytes 1064960 | tf_op jit(solution)/shard_map/all_gather | solution.py:103
  8.0 35.0 %copy-start.10 = (s32[4]{0:T(128)S(1)}, s32[4]{0:T(128)}, u32[]{:S(2)}) copy-start(s32[4]{0:T(128)} %param.9) | copy-start | bytes 52
  8.0 35.0 %copy-start.9 = (s32[4]{0:T(128)S(1)}, s32[4]{0:T(128)}, u32[]{:S(2)}) copy-start(s32[4]{0:T(128)} %param.8) | copy-start | bytes 52
  51.9 10.2 copy-start.8
  61.3 983.2 %all-reduce.3.cloned.1.call-start = ((), (), s32[]{:S(2)}) async-start(), calls=%async_computation.1 | async-start | bytes 2097152
  62.2 2.6 copy-start.7
  192.5 2.8 copy-start.1
  195.4 1.2 copy-start.2
  195.4 1.5 copy-start.3
  196.9 6.3 copy-start.4
  196.9 6.3 copy-start.5
  196.9 6.3 copy-start.6
  214.6 15.4 %collective-permute-start = (f32[4,1024]{1,0:T(4,128)S(1)}, f32[4,1024]{1,0:T(4,128)S(1)}, u32[]{:S(2)}, u32[]{:S(2)}) collective-permute-start(f32[4,1024]{1,0:T(4,128)S(1)} %get-tuple-element.13), channel_id=1, source_target_pairs={{0,64},{64,128},{128,192},{192,256},{256,320},{320,384},{384,448},... | collective-permute-start | bytes 49160 | tf_op jit(solution)/shard_map/ppermute | solution.py:13
Sparse Core Ops, SparseCore 0:
  61.4 125.8 all-gather.2
  214.7 829.7 all-reduce.2
where the time goes:
time: 1070 us
  waiting for transfers between devices  934 us (87%)
  matrix products  55.5 us (5%)
  local copies, waits for them, and re-layouts  45.2 us (4%)
  other arithmetic  19 us (2%)
  between operations  15.6 us (1%)
    unnamed x3, waiting for transfers between devices  813 us
    all_gather x1, waiting for transfers between devices, body(): group_spec = lax.all_gather(spectra, 'blk', axis=0, tiled=True)  111 us
    gather x2, local copies, waits for them, and re-layouts, taper_windows(): jnp.take_along_axis(records, starts[:, None] + sample[None, :], axis=1)  34.9 us
  transfers between devices with their start and end apart: 3, of which 3 were waited for; matrix products, arithmetic and copies ran while one was open for 2% of the time, Pallas kernels for 0%

commit v1 on v0

v1 whole, which is shorter than its diff:
```python
import jax
import jax.numpy as jnp
import ml_dtypes
import numpy as np
from jax import lax
from jax.experimental import pallas as pl
from jax.experimental.pallas import tpu as pltpu
from jax.sharding import PartitionSpec as P

WIN = 1024
HALF = 512
QUARTER = 256
TILE = 128
LANES = 128
F32 = jnp.float32
BF16 = jnp.bfloat16
MESH = pl.DeviceIdType.MESH
NY, NZ = 4, 8


def tables():
    t = np.arange(HALF)[:, None]
    parts = []
    for parity in (0, 1):
        k = 2 * np.arange(QUARTER)[None, :] + parity
        angle = 2.0 * np.pi * ((t * k) % WIN) / WIN
        full = np.concatenate([np.cos(angle), -np.sin(angle)], axis=1)
        high = full.astype(ml_dtypes.bfloat16)
        low = (full - high.astype(np.float64)).astype(ml_dtypes.bfloat16)
        parts += [high, low]
    return np.stack(parts)


def split(x):
    high = x.astype(BF16)
    return high, (x - high.astype(F32)).astype(BF16)


def dot_nn(a, b):
    return lax.dot_general(a, b, (((1,), (0,)), ((), ())), preferred_element_type=F32)


def dot_nt(a, b):
    return lax.dot_general(a, b, (((1,), (1,)), ((), ())), preferred_element_type=F32)


def dot3(dot, pair, high, low):
    return dot(pair[0], high) + dot(pair[1], high) + dot(pair[0], low)


def place():
    blk = lax.axis_index("blk")
    core = blk % 2
    z = (blk // 2) % NZ
    y = blk // (2 * NZ)
    sign = 1 - 2 * core
    return {
        "core": core,
        "z": z,
        "y": y,
        "up": (y + sign + NY) % NY,
        "down": (y - sign + NY) % NY,
        "across": (y + 2) % NY,
    }


def flip(z, d):
    out = 0
    for bit in (1, 2, 4):
        own = (z // bit) % 2
        out = out + bit * ((own + (d // bit) % 2) % 2)
    return out


def device(y, z, core):
    return y * (2 * NZ) + z * 2 + core


def slot_of(core, y, z):
    return (core * NY + y) * NZ + z


def enter(at):
    y, z, core = at["y"], at["z"], at["core"]
    peers = [device(y, z, 1 - core), device(at["up"], z, core), device(at["down"], z, core)]
    peers += [device(y, flip(z, d), core) for d in (1, 2, 3, 4)]
    barrier = pltpu.get_barrier_semaphore()
    for peer in peers:
        pl.semaphore_signal(barrier, inc=1, device_id={"blk": peer}, device_id_type=MESH)
    return barrier, len(peers)


def window_tiles(records, starts, tapers, stage):
    lane = lax.broadcasted_iota(jnp.int32, (8, LANES), 1)
    sample = lax.broadcasted_iota(jnp.int32, (8, LANES), 0) * LANES + lane
    position = sample.astype(F32)
    tiles = []
    for i in range(4):
        base = i * 16
        for c in range(16):
            stage[base + c : base + c + 1, :] = records[i : i + 1, c * LANES : (c + 1) * LANES]
        chunks = stage[base : base + 16, :]
        start = jnp.full((16, LANES), starts[i], jnp.int32)
        for bit in (1, 2, 4, 8):
            chunks = jnp.where(start & (bit * LANES) != 0, pltpu.roll(chunks, 16 - bit, 0), chunks)
        first, second = chunks[0:8, :], pltpu.roll(chunks, 15, 0)[0:8, :]
        start = start[0:8, :]
        for bit in (1, 2, 4, 8, 16, 32, 64):
            moved_first = pltpu.roll(first, LANES - bit, 1)
            moved_second = pltpu.roll(second, LANES - bit, 1)
            taken = start & bit != 0
            first = jnp.where(taken, jnp.where(lane < LANES - bit, moved_first, moved_second), first)
            second = jnp.where(taken, moved_second, second)
        length = jnp.full((8, LANES), tapers[i], jnp.int32).astype(F32)
        shape_fn = jnp.minimum(1.0, jnp.minimum((position + 1.0) / length, (WIN - position) / length))
        tiles.append(first * shape_fn * WIN ** (-0.25))
    return tiles


class Sender:
    def __init__(self, sems):
        self.sems, self.count, self.sent = sems, 0, []

    def __call__(self, src, dst, recv, target):
        copy = pltpu.make_async_remote_copy(
            src_ref=src,
            dst_ref=dst,
            send_sem=self.sems.at[self.count],
            recv_sem=recv,
            device_id=target,
            device_id_type=MESH,
        )
        copy.start()
        self.count += 1
        self.sent.append(copy)

    def drain(self):
        for copy in self.sent:
            copy.wait_send()


def arrived(dst, recv, sems, at):
    pltpu.make_async_remote_copy(
        src_ref=dst,
        dst_ref=dst,
        send_sem=sems.at[0],
        recv_sem=recv,
        device_id={"blk": device(at["y"], at["z"], 1 - at["core"])},
        device_id_type=MESH,
    ).wait_recv()


def gather_kernel(starts, tapers, records, group, near, stage, send_sems, recv_sems, far_sem):
    at = place()
    y, z, core = at["y"], at["z"], at["core"]
    region = lax.axis_index("region")
    regions = lax.axis_size("region")
    after, before = lax.rem(region + 1, regions), lax.rem(region + regions - 1, regions)
    barrier, count = enter(at)
    for other in (after, before):
        pl.semaphore_signal(barrier, inc=1, device_id={"region": other}, device_id_type=MESH)
    tiles = window_tiles(records, starts, tapers, stage)
    mine = slot_of(core, y, z)
    for i in range(4):
        group[pl.ds(pl.multiple_of(mine * 32, 32) + i * 8, 8), :] = tiles[i]
        near[i * 8 : i * 8 + 8, :] = tiles[i]
    pl.semaphore_wait(barrier, count + 2)

    send = Sender(send_sems)

    def rows(slot):
        return group.at[pl.ds(pl.multiple_of(slot * 32, 32), 32), :]

    def pass_on(slot, yy, zz, cc):
        send(rows(slot), rows(slot), recv_sems.at[slot], {"blk": device(yy, zz, cc)})

    def take(slot):
        arrived(rows(slot), recv_sems.at[slot], send_sems, at)

    def column(d):
        slot = slot_of(core, y, flip(z, d))
        if d:
            take(slot)
        if d == 0:
            for e in (4, 1, 2, 3):
                pass_on(slot, y, flip(z, e), core)
        if d == 4:
            for e in (1, 2, 3):
                pass_on(slot, y, flip(z, e), core)
        pass_on(slot, at["up"], z, core)
        pass_on(slot, at["down"], z, core)
        pass_on(slot, y, z, 1 - core)

    def beside(d):
        zz = flip(z, d)
        slot = slot_of(core, at["down"], zz)
        take(slot)
        pass_on(slot, at["up"], z, core)
        pass_on(slot, y, z, 1 - core)
        slot = slot_of(core, at["up"], zz)
        take(slot)
        pass_on(slot, y, z, 1 - core)

    def opposite(d):
        slot = slot_of(core, at["across"], flip(z, d))
        take(slot)
        pass_on(slot, y, z, 1 - core)

    column(0)
    send(near.at[0:32, :], near.at[32:64, :], far_sem.at[0], {"region": after})
    near_by, next_to, far_side = column, beside, opposite
    for step, d in (
        (near_by, 1), (next_to, 0), (near_by, 2), (near_by, 3), (next_to, 1), (far_side, 0), (near_by, 4),
        (next_to, 2), (far_side, 1), (next_to, 3), (far_side, 2), (next_to, 4), (near_by, 5), (far_side, 3),
        (near_by, 6), (near_by, 7), (next_to, 5), (far_side, 4), (next_to, 6), (next_to, 7), (far_side, 5),
        (far_side, 6), (far_side, 7),
    ):
        step(d)
    for yy in range(NY):
        for zz in range(NZ):
            take(slot_of(1 - core, yy, zz))
    arrived(near.at[32:64, :], far_sem.at[0], send_sems, at)
    send.drain()


def complex_parts(x):
    return x[:, :QUARTER], x[:, QUARTER:HALF], x[:, HALF : HALF + QUARTER], x[:, HALF + QUARTER :]


def spectra_of(tile_of, table):
    pieces = [tile_of(c) for c in range(8)]
    early = jnp.concatenate(pieces[:4], axis=1)
    late = jnp.concatenate(pieces[4:], axis=1)
    even = dot3(dot_nn, split(early + late), table[0], table[1])
    odd = dot3(dot_nn, split(early - late), table[2], table[3])
    return jnp.concatenate([even, odd], axis=1)


def cross(left, right):
    lr, li, mr, mi = complex_parts(left)
    rr, ri, sr, si = complex_parts(right)
    even = jnp.concatenate([lr * rr + li * ri, li * rr - lr * ri], axis=1)
    odd = jnp.concatenate([mr * sr + mi * si, mi * sr - mr * si], axis=1)
    return even, odd


def halve_first(x):
    lane = lax.broadcasted_iota(jnp.int32, (1, HALF), 1)
    return x * jnp.where(lane == 0, 0.5, 1.0).astype(F32)


def spread(row):
    return jnp.broadcast_to(row, (LANES, LANES)).T


def pairs_kernel(
    count, group, near, pair_a, pair_b, observed, table, corr, remote, local, far, spec, own, conj_terms, plain_terms
):
    slots = corr.shape[0]
    spectra = spectra_of(lambda c: group[pl.ds(c, QUARTER, stride=8), :], table)
    high, low = split(spectra)
    spec[0:QUARTER, :] = high
    spec[QUARTER:HALF, :] = low
    ends = spectra_of(lambda c: near[pl.ds(c, 8, stride=8), :], table)
    own[...] = ends
    far_even, far_odd = cross(ends[0:4, :], ends[4:8, :])
    far[...] = jnp.concatenate([halve_first(far_even), far_odd], axis=1)
    live_count = count[0]
    lane = lax.broadcasted_iota(jnp.int32, (TILE, LANES), 1)

    def tile(i, carry):
        rows = pl.ds(pl.multiple_of(i * TILE, TILE), TILE)
        low_rows = pl.ds(pl.multiple_of(slots + i * TILE, TILE), TILE)
        b_col = spread(pair_b[pl.ds(i, 1), :])
        a_col = spread(pair_a[pl.ds(i, 1), :])
        hot = jnp.concatenate([b_col == lane, b_col == lane + LANES], axis=1).astype(F32).astype(BF16)
        target = dot_nn(hot, spec[0:QUARTER, :]) + dot_nn(hot, spec[QUARTER:HALF, :])
        pieces = []
        for c in range(8):
            cut = slice(c * LANES, (c + 1) * LANES)
            row = [jnp.broadcast_to(own[q : q + 1, cut], (TILE, LANES)) for q in range(4)]
            pieces.append(
                jnp.where(a_col == 0, row[0], jnp.where(a_col == 1, row[1], jnp.where(a_col == 2, row[2], row[3])))
            )
        source = jnp.concatenate(pieces, axis=1)
        even, odd = cross(source, target)
        lag_even = dot3(dot_nt, split(halve_first(even)), table[0], table[1])
        lag_odd = dot3(dot_nt, split(odd), table[2], table[3])
        ahead = (lag_even[:, :QUARTER] + lag_odd[:, :QUARTER]) * (2.0 / WIN)
        behind = (lag_even[:, QUARTER:] - lag_odd[:, QUARTER:]) * (2.0 / WIN)
        number = lax.broadcasted_iota(jnp.int32, (TILE, QUARTER), 0) + i * TILE
        live = number < live_count
        corr[rows, 0:QUARTER] = jnp.where(live, behind, 0.0)
        corr[rows, QUARTER:HALF] = jnp.where(live, ahead, 0.0)
        res_behind = split(jnp.where(live, behind - observed[rows, 0:QUARTER], 0.0))
        res_ahead = split(jnp.where(live, ahead - observed[rows, QUARTER:HALF], 0.0))
        plus = [jnp.concatenate([res_ahead[q], res_behind[q]], axis=1) for q in (0, 1)]
        minus = [jnp.concatenate([res_ahead[q], -res_behind[q]], axis=1) for q in (0, 1)]
        mis_even = dot3(dot_nn, plus, table[0], table[1])
        mis_odd = dot3(dot_nn, minus, table[2], table[3])
        for p, mis in ((0, mis_even), (1, mis_odd)):
            mr, mi = mis[:, :QUARTER], mis[:, QUARTER:]
            base = p * HALF
            sr, si = source[:, base : base + QUARTER], source[:, base + QUARTER : base + HALF]
            tr, ti = target[:, base : base + QUARTER], target[:, base + QUARTER : base + HALF]
            for terms, re, im in (
                (conj_terms, mr * sr + mi * si, mr * si - mi * sr),
                (plain_terms, mr * tr - mi * ti, mr * ti + mi * tr),
            ):
                for offset, part in ((0, re), (QUARTER, im)):
                    part_high, part_low = split(part)
                    cut = slice(base + offset, base + offset + QUARTER)
                    terms[rows, cut] = part_high
                    terms[low_rows, cut] = part_low
        return carry

    lax.fori_loop(0, slots // TILE, tile, 0)

    def hot_rows(index, height):
        down = lax.broadcasted_iota(jnp.int32, (height, LANES), 0)
        cols = [
            (jnp.broadcast_to(index[i : i + 1, :], (height, LANES)) == down).astype(F32).astype(BF16)
            for i in range(slots // LANES)
        ]
        return jnp.concatenate(cols + cols, axis=1)

    totals = dot_nn(hot_rows(pair_b, QUARTER), conj_terms[...])
    own_totals = dot_nn(hot_rows(pair_a, 8), plain_terms[...])
    for c in range(8):
        remote[pl.ds(c, QUARTER, stride=8), :] = totals[:, c * LANES : (c + 1) * LANES]
    local[...] = own_totals


def reduce_kernel(
    remote, local, far, table, adjoint, far_corr, plane_in, across_in, up_in, down_in, relay_in, mate_in, cross_in,
    total, sums, send_sems, plane_sems, ring_sems, mate_sems,
):
    at = place()
    y, z, core = at["y"], at["z"], at["core"]
    barrier, count = enter(at)
    pl.semaphore_wait(barrier, count)
    send = Sender(send_sems)
    half = z // 4

    def part(cc, yy, zz, n):
        return pl.ds(pl.multiple_of(slot_of(cc, yy, zz) * 32, 32), n * 32)

    def plane(yy):
        return pl.ds(pl.multiple_of(yy * (NZ * 32), NZ * 32), NZ * 32)

    for yy in (at["across"], at["up"], at["down"], y):
        send(
            remote.at[part(1 - core, yy, 0, NZ), :],
            plane_in.at[plane(yy), :],
            plane_sems.at[yy],
            {"blk": device(y, z, 1 - core)},
        )

    def add_plane(yy):
        arrived(plane_in.at[plane(yy), :], plane_sems.at[yy], send_sems, at)
        sums[plane(yy), :] = remote[part(core, yy, 0, NZ), :] + plane_in[plane(yy), :]

    def piece(yy, zz, n):
        return pl.ds(pl.multiple_of((yy * NZ + zz) * 32, 32), n * 32)

    def halves():
        return ((0, 1 - half), (1, half))

    def ring(k, h):
        return pl.ds(pl.multiple_of(h * 128, 128), 128)

    up = {"blk": device(at["up"], z, core)}
    down = {"blk": device(at["down"], z, core)}
    add_plane(at["across"])
    for k, h in halves():
        send(sums.at[piece(at["across"], h * 4, 4), :], across_in.at[ring(k, h), :], ring_sems.at[k], up)
    add_plane(at["down"])
    for k, h in halves():
        send(sums.at[piece(at["down"], h * 4, 4), :], down_in.at[ring(k, h), :], ring_sems.at[2 + k], down)
    add_plane(at["up"])
    for k, h in halves():
        arrived(across_in.at[ring(k, h), :], ring_sems.at[k], send_sems, at)
        rows = piece(at["up"], h * 4, 4)
        sums[rows, :] = sums[rows, :] + across_in[ring(k, h), :]
        send(sums.at[rows, :], up_in.at[ring(k, h), :], ring_sems.at[4 + k], up)
    add_plane(y)

    def block(d):
        return piece(y, flip(z, d), 1)

    for k, h in halves():
        arrived(down_in.at[ring(k, h), :], ring_sems.at[2 + k], send_sems, at)
        arrived(up_in.at[ring(k, h), :], ring_sems.at[4 + k], send_sems, at)
        rows = piece(y, h * 4, 4)
        sums[rows, :] = sums[rows, :] + (down_in[ring(k, h), :] + up_in[ring(k, h), :])
        bucket, base, first = (relay_in, 0, 4) if k == 0 else (mate_in, 4, 0)
        for j in (1, 2, 3):
            send(
                sums.at[block(first + j), :],
                bucket.at[(j - 1) * 32 : j * 32, :],
                mate_sems.at[base + j - 1],
                {"blk": device(y, flip(z, j), core)},
            )
    for j in (1, 2, 3):
        arrived(relay_in.at[(j - 1) * 32 : j * 32, :], mate_sems.at[j - 1], send_sems, at)
    total[0:32, :] = (
        sums[block(4), :] + relay_in[0:32, :] + (relay_in[32:64, :] + relay_in[64:96, :])
    )
    send(total.at[0:32, :], cross_in, mate_sems.at[3], {"blk": device(y, flip(z, 4), core)})
    for j in (1, 2, 3):
        arrived(mate_in.at[(j - 1) * 32 : j * 32, :], mate_sems.at[4 + j - 1], send_sems, at)
    summed = sums[block(0), :] + mate_in[0:32, :] + (mate_in[32:64, :] + mate_in[64:96, :])
    arrived(cross_in, mate_sems.at[3], send_sems, at)
    total[32:64, :] = summed + cross_in[...]

    pieces = [total[pl.ds(32 + c, 4, stride=8), :] for c in range(8)]
    source = jnp.concatenate(pieces, axis=1) + local[0:4, :]
    even = jnp.concatenate([halve_first(source[:, :HALF]), far[:, :HALF]], axis=0)
    odd = jnp.concatenate([source[:, HALF:], far[:, HALF:]], axis=0)
    lag_even = dot3(dot_nt, split(even), table[0], table[1])
    lag_odd = dot3(dot_nt, split(odd), table[2], table[3])
    plus = (lag_even + lag_odd) * (2.0 / WIN)
    minus = (lag_even - lag_odd) * (2.0 / WIN)
    adjoint[:, :HALF] = plus[0:4, :] * (1.0 / 16.0)
    adjoint[:, HALF:] = minus[0:4, :] * (1.0 / 16.0)
    far_corr[:, :QUARTER] = minus[4:8, QUARTER:]
    far_corr[:, QUARTER:] = plus[4:8, :QUARTER]
    send.drain()


def vmem():
    return pl.BlockSpec(memory_space=pltpu.VMEM)


def smem():
    return pl.BlockSpec(memory_space=pltpu.SMEM)


def params(**kw):
    return pltpu.CompilerParams(vmem_limit_bytes=56 * 1024 * 1024, **kw)


def body(records, starts, tapers, pair_a, pair_b, pair_count, observed):
    slots = pair_a.shape[0]
    shape = jax.ShapeDtypeStruct
    table = jnp.asarray(tables())
    group, near = pl.pallas_call(
        gather_kernel,
        out_shape=(shape((2048, LANES), F32), shape((64, LANES), F32)),
        in_specs=[smem(), smem(), vmem()],
        out_specs=(vmem(), vmem()),
        scratch_shapes=[
            pltpu.VMEM((64, LANES), F32),
            pltpu.SemaphoreType.DMA((72,)),
            pltpu.SemaphoreType.DMA((64,)),
            pltpu.SemaphoreType.DMA((1,)),
        ],
        compiler_params=params(collective_id=0, has_side_effects=True),
        name="gather_windows",
    )(starts, tapers, records)
    placed = (pair_b // 4 % 2) * 128 + (pair_b // 8) * 4 + pair_b % 4
    corr, remote, local, far = pl.pallas_call(
        pairs_kernel,
        out_shape=(
            shape((slots, HALF), F32),
            shape((2048, LANES), F32),
            shape((8, WIN), F32),
            shape((4, WIN), F32),
        ),
        in_specs=[smem()] + [vmem()] * 6,
        out_specs=(vmem(),) * 4,
        scratch_shapes=[
            pltpu.VMEM((HALF, WIN), BF16),
            pltpu.VMEM((8, WIN), F32),
            pltpu.VMEM((2 * slots, WIN), BF16),
            pltpu.VMEM((2 * slots, WIN), BF16),
        ],
        compiler_params=params(),
        name="pairs",
    )(
        pair_count,
        group,
        near,
        pair_a.reshape(slots // LANES, LANES),
        placed.reshape(slots // LANES, LANES),
        observed,
        table,
    )
    adjoint, far_corr = pl.pallas_call(
        reduce_kernel,
        out_shape=(shape((4, WIN), F32), shape((4, HALF), F32)),
        in_specs=[vmem()] * 4,
        out_specs=(vmem(), vmem()),
        scratch_shapes=[
            pltpu.VMEM((1024, LANES), F32),
            pltpu.VMEM((256, LANES), F32),
            pltpu.VMEM((256, LANES), F32),
            pltpu.VMEM((256, LANES), F32),
            pltpu.VMEM((96, LANES), F32),
            pltpu.VMEM((96, LANES), F32),
            pltpu.VMEM((32, LANES), F32),
            pltpu.VMEM((64, LANES), F32),
            pltpu.VMEM((1024, LANES), F32),
            pltpu.SemaphoreType.DMA((24,)),
            pltpu.SemaphoreType.DMA((4,)),
            pltpu.SemaphoreType.DMA((6,)),
            pltpu.SemaphoreType.DMA((7,)),
        ],
        compiler_params=params(collective_id=1, has_side_effects=True),
        name="reduce_terms",
    )(remote, local, far, table)
    return corr, far_corr, adjoint


def solution(mesh):
    split_all = P(("region", "blk"))
    rows = P(("region", "blk"), None)
    return jax.shard_map(
        body,
        mesh=mesh,
        in_specs=(rows, split_all, split_all, split_all, split_all, split_all, rows),
        out_specs=(rows, rows, rows),
        check_vma=False,
    )
```

time: 1070 us -> 89.2 us (0.08)
  the two profiles are of different devices: /device:TPU:1 before, /device:TPU:16 now
where the time goes in v1:
time: 89.2 us; the launch traced here: 88.9 us
  Pallas kernels  83.7 us (94%)
  local copies, waits for them, and re-layouts  2.62 us (3%)
  other arithmetic  1.3 us (1%)
  between operations  1.29 us (1%)
    pallas_call x1, Pallas kernels, body(): pl.pallas_call(gather_kernel, out_shape=(shape((2048, LANES), F32), shape...  38 us
    pallas_call x1, Pallas kernels, body(): pl.pallas_call(reduce_kernel, out_shape=(shape((4, WIN), F32), shape((4,...  26.6 us
    pallas_call x1, Pallas kernels, body(): pl.pallas_call(pairs_kernel, out_shape=(shape((slots, HALF), F32), shape(...  19.1 us
    unnamed x2, local copies, waits for them, and re-layouts  2.62 us

profile of v1, /device:TPU:16, one launch (start us, length us, event | category | flops | bytes accessed | tf_op | source)
XLA Modules:
  0.0 88.9 jit_solution(15657713388180176335)
XLA Ops:
  1.3 1.3 %fusion.4.pair_b = s32[6,128]{1,0:T(8,128)} fusion(s32[768]{0:T(1024)} %param.12), kind=kLoop, calls=%fused_computation.15 | loop fusion | flops 33792 | bytes 6144 | tf_op jit(solution)/shard_map/reshape | solution.py:485
  2.6 38.0 %gather_windows.1 = (f32[2048,128]{1,0:T(8,128)}, f32[64,128]{1,0:T(8,128)}) custom-call(s32[4]{0:T(128)} %starts.1, s32[4]{0:T(128)} %tapers.1, f32[4,2048]{1,0:T(4,128)} %records.1), custom_call_target="tpu_custom_call" | custom-call | tf_op jit(solution)/shard_map/gather_windows/pallas_call | solution.py:447
  40.5 19.1 %pairs.1 = (f32[768,512]{1,0:T(8,128)}, f32[2048,128]{1,0:T(8,128)}, f32[8,1024]{1,0:T(8,128)}, f32[4,1024]{1,0:T(4,128)}) custom-call(s32[1]{0:T(128)S(6)} %copy.13.count, f32[2048,128]{1,0:T(8,128)} %get-tuple-element.11.group, f32[64,128]{1,0:T(8,128)} %get-tuple-element.12.near, s32[6,128]{1,0:T(8,128)} %bitcast.3, s32[6,128]{1,0:T(8,128)} %fusion.4.pair_b, ...), custom_call_target="tpu_custom_call" | custom-call | tf_op jit(solution)/shard_map/pairs/pallas_call | solution.py:462
  59.7 26.6 %reduce_terms.1 = (f32[4,1024]{1,0:T(4,128)}, f32[4,512]{1,0:T(4,128)}) custom-call(f32[2048,128]{1,0:T(8,128)} %get-tuple-element.14.remote, f32[8,1024]{1,0:T(8,128)} %get-tuple-element.15.local, f32[4,1024]{1,0:T(4,128)} %get-tuple-element.16.far, bf16[4,512,512]{2,1,0:T(8,128)(2,1)} %constant.52.clone.table), custom_call_target="tpu_custom_call" | custom-call | tf_op jit(solution)/shard_map/reduce_terms/pallas_call | solution.py:489
  86.2 1.3 %copy.14 = f32[4,512]{1,0:T(4,128)} copy(f32[4,512]{1,0:T(4,128)} %get-tuple-element.23) | data formatting | bytes 16384
  87.5 1.3 %copy.15 = f32[4,1024]{1,0:T(4,128)} copy(f32[4,1024]{1,0:T(4,128)} %get-tuple-element.24) | data formatting | bytes 32768

commit v2 on v1

--- a/solution.py
+++ b/solution.py
@@ -53,15 +53,7 @@
     core = blk % 2
     z = (blk // 2) % NZ
     y = blk // (2 * NZ)
-    sign = 1 - 2 * core
-    return {
-        "core": core,
-        "z": z,
-        "y": y,
-        "up": (y + sign + NY) % NY,
-        "down": (y - sign + NY) % NY,
-        "across": (y + 2) % NY,
-    }
+    return {"core": core, "z": z, "y": y}
 
 
 def flip(z, d):
@@ -76,14 +68,19 @@
     return y * (2 * NZ) + z * 2 + core
 
 
-def slot_of(core, y, z):
-    return (core * NY + y) * NZ + z
+def slot_of(core, z, y):
+    return (core * NZ + z) * NY + y
+
+
+def turn(y, k):
+    return (y + k) % NY
 
 
 def enter(at):
     y, z, core = at["y"], at["z"], at["core"]
-    peers = [device(y, z, 1 - core), device(at["up"], z, core), device(at["down"], z, core)]
-    peers += [device(y, flip(z, d), core) for d in (1, 2, 3, 4)]
+    peers = [device(y, z, 1 - core)]
+    peers += [device(turn(y, k), z, core) for k in (1, 2, 3)]
+    peers += [device(y, flip(z, d), core) for d in range(1, NZ)]
     barrier = pltpu.get_barrier_semaphore()
     for peer in peers:
         pl.semaphore_signal(barrier, inc=1, device_id={"blk": peer}, device_id_type=MESH)
@@ -160,7 +157,7 @@
     for other in (after, before):
         pl.semaphore_signal(barrier, inc=1, device_id={"region": other}, device_id_type=MESH)
     tiles = window_tiles(records, starts, tapers, stage)
-    mine = slot_of(core, y, z)
+    mine = slot_of(core, z, y)
     for i in range(4):
         group[pl.ds(pl.multiple_of(mine * 32, 32) + i * 8, 8), :] = tiles[i]
         near[i * 8 : i * 8 + 8, :] = tiles[i]
@@ -177,48 +174,24 @@
     def take(slot):
         arrived(rows(slot), recv_sems.at[slot], send_sems, at)
 
-    def column(d):
-        slot = slot_of(core, y, flip(z, d))
+    for d in (7, 6, 5, 4, 3, 2, 1):
+        pass_on(mine, y, flip(z, d), core)
+    for d in range(NZ):
+        slot = slot_of(core, flip(z, d), y)
         if d:
             take(slot)
-        if d == 0:
-            for e in (4, 1, 2, 3):
-                pass_on(slot, y, flip(z, e), core)
-        if d == 4:
-            for e in (1, 2, 3):
-                pass_on(slot, y, flip(z, e), core)
-        pass_on(slot, at["up"], z, core)
-        pass_on(slot, at["down"], z, core)
+        for k in (2, 1, 3):
+            pass_on(slot, turn(y, k), z, core)
         pass_on(slot, y, z, 1 - core)
-
-    def beside(d):
-        zz = flip(z, d)
-        slot = slot_of(core, at["down"], zz)
-        take(slot)
-        pass_on(slot, at["up"], z, core)
-        pass_on(slot, y, z, 1 - core)
-        slot = slot_of(core, at["up"], zz)
-        take(slot)
-        pass_on(slot, y, z, 1 - core)
-
-    def opposite(d):
-        slot = slot_of(core, at["across"], flip(z, d))
-        take(slot)
-        pass_on(slot, y, z, 1 - core)
-
-    column(0)
     send(near.at[0:32, :], near.at[32:64, :], far_sem.at[0], {"region": after})
-    near_by, next_to, far_side = column, beside, opposite
-    for step, d in (
-        (near_by, 1), (next_to, 0), (near_by, 2), (near_by, 3), (next_to, 1), (far_side, 0), (near_by, 4),
-        (next_to, 2), (far_side, 1), (next_to, 3), (far_side, 2), (next_to, 4), (near_by, 5), (far_side, 3),
-        (near_by, 6), (near_by, 7), (next_to, 5), (far_side, 4), (next_to, 6), (next_to, 7), (far_side, 5),
-        (far_side, 6), (far_side, 7),
-    ):
-        step(d)
-    for yy in range(NY):
-        for zz in range(NZ):
-            take(slot_of(1 - core, yy, zz))
+    for d in range(NZ):
+        for k in (1, 3, 2):
+            slot = slot_of(core, flip(z, d), turn(y, k))
+            take(slot)
+            pass_on(slot, y, z, 1 - core)
+    for zz in range(NZ):
+        for yy in range(NY):
+            take(slot_of(1 - core, zz, yy))
     arrived(near.at[32:64, :], far_sem.at[0], send_sems, at)
     send.drain()
 
@@ -332,88 +305,64 @@
 
 
 def reduce_kernel(
-    remote, local, far, table, adjoint, far_corr, plane_in, across_in, up_in, down_in, relay_in, mate_in, cross_in,
-    total, sums, send_sems, plane_sems, ring_sems, mate_sems,
+    remote, local, far, table, adjoint, far_corr, plane_in, ring_in, mate_in, sums, total,
+    send_sems, plane_sems, ring_sems, mate_sems,
 ):
     at = place()
     y, z, core = at["y"], at["z"], at["core"]
     barrier, count = enter(at)
     pl.semaphore_wait(barrier, count)
     send = Sender(send_sems)
-    half = z // 4
-
-    def part(cc, yy, zz, n):
-        return pl.ds(pl.multiple_of(slot_of(cc, yy, zz) * 32, 32), n * 32)
-
-    def plane(yy):
-        return pl.ds(pl.multiple_of(yy * (NZ * 32), NZ * 32), NZ * 32)
-
-    for yy in (at["across"], at["up"], at["down"], y):
+    outward = (7, 6, 5, 4, 3, 2, 1, 0)
+
+    def part(cc, zz):
+        return pl.ds(pl.multiple_of(slot_of(cc, zz, 0) * 32, 32), NY * 32)
+
+    def block(zz, yy):
+        return pl.ds(pl.multiple_of(slot_of(0, zz, yy) * 32, 32), 32)
+
+    def ring(k, d):
+        return slice(((k - 1) * NZ + d) * 32, ((k - 1) * NZ + d + 1) * 32)
+
+    def mate(d):
+        return slice(d * 32, d * 32 + 32)
+
+    for d in outward:
+        zz = flip(z, d)
         send(
-            remote.at[part(1 - core, yy, 0, NZ), :],
-            plane_in.at[plane(yy), :],
-            plane_sems.at[yy],
+            remote.at[part(1 - core, zz), :],
+            plane_in.at[part(0, zz), :],
+            plane_sems.at[d],
             {"blk": device(y, z, 1 - core)},
         )
-
-    def add_plane(yy):
-        arrived(plane_in.at[plane(yy), :], plane_sems.at[yy], send_sems, at)
-        sums[plane(yy), :] = remote[part(core, yy, 0, NZ), :] + plane_in[plane(yy), :]
-
-    def piece(yy, zz, n):
-        return pl.ds(pl.multiple_of((yy * NZ + zz) * 32, 32), n * 32)
-
-    def halves():
-        return ((0, 1 - half), (1, half))
-
-    def ring(k, h):
-        return pl.ds(pl.multiple_of(h * 128, 128), 128)
-
-    up = {"blk": device(at["up"], z, core)}
-    down = {"blk": device(at["down"], z, core)}
-    add_plane(at["across"])
-    for k, h in halves():
-        send(sums.at[piece(at["across"], h * 4, 4), :], across_in.at[ring(k, h), :], ring_sems.at[k], up)
-    add_plane(at["down"])
-    for k, h in halves():
-        send(sums.at[piece(at["down"], h * 4, 4), :], down_in.at[ring(k, h), :], ring_sems.at[2 + k], down)
-    add_plane(at["up"])
-    for k, h in halves():
-        arrived(across_in.at[ring(k, h), :], ring_sems.at[k], send_sems, at)
-        rows = piece(at["up"], h * 4, 4)
-        sums[rows, :] = sums[rows, :] + across_in[ring(k, h), :]
-        send(sums.at[rows, :], up_in.at[ring(k, h), :], ring_sems.at[4 + k], up)
-    add_plane(y)
-
-    def block(d):
-        return piece(y, flip(z, d), 1)
-
-    for k, h in halves():
-        arrived(down_in.at[ring(k, h), :], ring_sems.at[2 + k], send_sems, at)
-        arrived(up_in.at[ring(k, h), :], ring_sems.at[4 + k], send_sems, at)
-        rows = piece(y, h * 4, 4)
-        sums[rows, :] = sums[rows, :] + (down_in[ring(k, h), :] + up_in[ring(k, h), :])
-        bucket, base, first = (relay_in, 0, 4) if k == 0 else (mate_in, 4, 0)
-        for j in (1, 2, 3):
+    for d in outward:
+        zz = flip(z, d)
+        arrived(plane_in.at[part(0, zz), :], plane_sems.at[d], send_sems, at)
+        sums[part(0, zz), :] = remote[part(core, zz), :] + plane_in[part(0, zz), :]
+        for k in (2, 1, 3):
             send(
-                sums.at[block(first + j), :],
-                bucket.at[(j - 1) * 32 : j * 32, :],
-                mate_sems.at[base + j - 1],
-                {"blk": device(y, flip(z, j), core)},
+                sums.at[block(zz, turn(y, k)), :],
+                ring_in.at[ring(k, d), :],
+                ring_sems.at[(k - 1) * NZ + d],
+                {"blk": device(turn(y, k), z, core)},
             )
-    for j in (1, 2, 3):
-        arrived(relay_in.at[(j - 1) * 32 : j * 32, :], mate_sems.at[j - 1], send_sems, at)
-    total[0:32, :] = (
-        sums[block(4), :] + relay_in[0:32, :] + (relay_in[32:64, :] + relay_in[64:96, :])
-    )
-    send(total.at[0:32, :], cross_in, mate_sems.at[3], {"blk": device(y, flip(z, 4), core)})
-    for j in (1, 2, 3):
-        arrived(mate_in.at[(j - 1) * 32 : j * 32, :], mate_sems.at[4 + j - 1], send_sems, at)
-    summed = sums[block(0), :] + mate_in[0:32, :] + (mate_in[32:64, :] + mate_in[64:96, :])
-    arrived(cross_in, mate_sems.at[3], send_sems, at)
-    total[32:64, :] = summed + cross_in[...]
-
-    pieces = [total[pl.ds(32 + c, 4, stride=8), :] for c in range(8)]
+    for d in outward:
+        for k in (1, 3, 2):
+            arrived(ring_in.at[ring(k, d), :], ring_sems.at[(k - 1) * NZ + d], send_sems, at)
+        total[mate(d), :] = (
+            sums[block(flip(z, d), y), :] + ring_in[ring(1, d), :] + (ring_in[ring(2, d), :] + ring_in[ring(3, d), :])
+        )
+        if d:
+            send(
+                total.at[mate(d), :], mate_in.at[mate(d), :], mate_sems.at[d], {"blk": device(y, flip(z, d), core)}
+            )
+    summed = total[mate(0), :]
+    for d in (1, 2, 3, 4, 5, 6, 7):
+        arrived(mate_in.at[mate(d), :], mate_sems.at[d], send_sems, at)
+        summed = summed + mate_in[mate(d), :]
+    total[mate(0), :] = summed
+
+    pieces = [total[pl.ds(c, 4, stride=8), :] for c in range(8)]
     source = jnp.concatenate(pieces, axis=1) + local[0:4, :]
     even = jnp.concatenate([halve_first(source[:, :HALF]), far[:, :HALF]], axis=0)
     odd = jnp.concatenate([source[:, HALF:], far[:, HALF:]], axis=0)
@@ -458,7 +407,7 @@
         compiler_params=params(collective_id=0, has_side_effects=True),
         name="gather_windows",
     )(starts, tapers, records)
-    placed = (pair_b // 4 % 2) * 128 + (pair_b // 8) * 4 + pair_b % 4
+    placed = (pair_b // 4 % 2) * 128 + (pair_b // 8 % NZ) * 16 + (pair_b // 64) * 4 + pair_b % 4
     corr, remote, local, far = pl.pallas_call(
         pairs_kernel,
         out_shape=(
@@ -493,18 +442,14 @@
         out_specs=(vmem(), vmem()),
         scratch_shapes=[
             pltpu.VMEM((1024, LANES), F32),
+            pltpu.VMEM((768, LANES), F32),
             pltpu.VMEM((256, LANES), F32),
+            pltpu.VMEM((1024, LANES), F32),
             pltpu.VMEM((256, LANES), F32),
-            pltpu.VMEM((256, LANES), F32),
-            pltpu.VMEM((96, LANES), F32),
-            pltpu.VMEM((96, LANES), F32),
-            pltpu.VMEM((32, LANES), F32),
-            pltpu.VMEM((64, LANES), F32),
-            pltpu.VMEM((1024, LANES), F32),
+            pltpu.SemaphoreType.DMA((40,)),
+            pltpu.SemaphoreType.DMA((8,)),
             pltpu.SemaphoreType.DMA((24,)),
-            pltpu.SemaphoreType.DMA((4,)),
-            pltpu.SemaphoreType.DMA((6,)),
-            pltpu.SemaphoreType.DMA((7,)),
+            pltpu.SemaphoreType.DMA((8,)),
         ],
         compiler_params=params(collective_id=1, has_side_effects=True),
         name="reduce_terms",

time: 89.2 us -> 82.2 us (0.922)
  the two profiles are of different devices: /device:TPU:16 before, /device:TPU:1 now
where the time goes in v2:
time: 82.2 us; the launch traced here: 81.8 us
  Pallas kernels  76.6 us (93%)
  local copies, waits for them, and re-layouts  2.62 us (3%)
  other arithmetic  1.3 us (2%)
  between operations  1.29 us (2%)
    pallas_call x1, Pallas kernels, body(): pl.pallas_call(gather_kernel, out_shape=(shape((2048, LANES), F32), shape...  36.5 us
    pallas_call x1, Pallas kernels, body(): pl.pallas_call(reduce_kernel, out_shape=(shape((4, WIN), F32), shape((4,...  21 us
    pallas_call x1, Pallas kernels, body(): pl.pallas_call(pairs_kernel, out_shape=(shape((slots, HALF), F32), shape(...  19.1 us
    unnamed x2, local copies, waits for them, and re-layouts  2.62 us

profile of v2, /device:TPU:1, one launch (start us, length us, event | category | flops | bytes accessed | tf_op | source)
XLA Modules:
  0.0 81.8 jit_solution(17974708860052535504)
XLA Ops:
  1.3 1.3 %fusion.5.pair_b = s32[6,128]{1,0:T(8,128)} fusion(s32[768]{0:T(1024)} %param.12), kind=kLoop, calls=%fused_computation.22 | loop fusion | flops 51456 | bytes 6144 | tf_op jit(solution)/shard_map/reshape | solution.py:434
  2.6 36.5 %gather_windows.1 = (f32[2048,128]{1,0:T(8,128)}, f32[64,128]{1,0:T(8,128)}) custom-call(s32[4]{0:T(128)} %starts.1, s32[4]{0:T(128)} %tapers.1, f32[4,2048]{1,0:T(4,128)} %records.1), custom_call_target="tpu_custom_call" | custom-call | tf_op jit(solution)/shard_map/gather_windows/pallas_call | solution.py:396
  39.1 19.1 %pairs.1 = (f32[768,512]{1,0:T(8,128)}, f32[2048,128]{1,0:T(8,128)}, f32[8,1024]{1,0:T(8,128)}, f32[4,1024]{1,0:T(4,128)}) custom-call(s32[1]{0:T(128)S(6)} %copy.13.count, f32[2048,128]{1,0:T(8,128)} %get-tuple-element.11.group, f32[64,128]{1,0:T(8,128)} %get-tuple-element.12.near, s32[6,128]{1,0:T(8,128)} %bitcast.3, s32[6,128]{1,0:T(8,128)} %fusion.5.pair_b, ...), custom_call_target="tpu_custom_call" | custom-call | tf_op jit(solution)/shard_map/pairs/pallas_call | solution.py:411
  58.2 21.0 %reduce_terms.1 = (f32[4,1024]{1,0:T(4,128)}, f32[4,512]{1,0:T(4,128)}) custom-call(f32[2048,128]{1,0:T(8,128)} %get-tuple-element.14.remote, f32[8,1024]{1,0:T(8,128)} %get-tuple-element.15.local, f32[4,1024]{1,0:T(4,128)} %get-tuple-element.16.far, bf16[4,512,512]{2,1,0:T(8,128)(2,1)} %constant.74.clone.table), custom_call_target="tpu_custom_call" | custom-call | tf_op jit(solution)/shard_map/reduce_terms/pallas_call | solution.py:438
  79.2 1.3 %copy.14 = f32[4,512]{1,0:T(4,128)} copy(f32[4,512]{1,0:T(4,128)} %get-tuple-element.23) | data formatting | bytes 16384
  80.5 1.3 %copy.15 = f32[4,1024]{1,0:T(4,128)} copy(f32[4,1024]{1,0:T(4,128)} %get-tuple-element.24) | data formatting | bytes 32768

commit v3 on v2

--- a/solution.py
+++ b/solution.py
@@ -10,7 +10,7 @@
 WIN = 1024
 HALF = 512
 QUARTER = 256
-TILE = 128
+TILE = 768
 LANES = 128
 F32 = jnp.float32
 BF16 = jnp.bfloat16
@@ -19,16 +19,15 @@
 
 
 def tables():
-    t = np.arange(HALF)[:, None]
-    parts = []
-    for parity in (0, 1):
-        k = 2 * np.arange(QUARTER)[None, :] + parity
-        angle = 2.0 * np.pi * ((t * k) % WIN) / WIN
+    def table(t, k):
+        angle = 2.0 * np.pi * ((t[:, None] * k[None, :]) % WIN) / WIN
         full = np.concatenate([np.cos(angle), -np.sin(angle)], axis=1)
         high = full.astype(ml_dtypes.bfloat16)
-        low = (full - high.astype(np.float64)).astype(ml_dtypes.bfloat16)
-        parts += [high, low]
-    return np.stack(parts)
+        return [high, (full - high.astype(np.float64)).astype(ml_dtypes.bfloat16)]
+
+    four = 4 * np.arange(LANES)
+    quarter = np.stack(table(np.arange(QUARTER), four) + table(np.arange(QUARTER), four + 2))
+    return quarter, np.stack(table(np.arange(HALF), 2 * np.arange(QUARTER) + 1))
 
 
 def split(x):
@@ -147,21 +146,16 @@
     ).wait_recv()
 
 
-def gather_kernel(starts, tapers, records, group, near, stage, send_sems, recv_sems, far_sem):
+def gather_kernel(starts, tapers, records, group, near, stage, send_sems, recv_sems):
     at = place()
     y, z, core = at["y"], at["z"], at["core"]
-    region = lax.axis_index("region")
-    regions = lax.axis_size("region")
-    after, before = lax.rem(region + 1, regions), lax.rem(region + regions - 1, regions)
     barrier, count = enter(at)
-    for other in (after, before):
-        pl.semaphore_signal(barrier, inc=1, device_id={"region": other}, device_id_type=MESH)
     tiles = window_tiles(records, starts, tapers, stage)
     mine = slot_of(core, z, y)
     for i in range(4):
         group[pl.ds(pl.multiple_of(mine * 32, 32) + i * 8, 8), :] = tiles[i]
         near[i * 8 : i * 8 + 8, :] = tiles[i]
-    pl.semaphore_wait(barrier, count + 2)
+    pl.semaphore_wait(barrier, count)
 
     send = Sender(send_sems)
 
@@ -183,7 +177,6 @@
         for k in (2, 1, 3):
             pass_on(slot, turn(y, k), z, core)
         pass_on(slot, y, z, 1 - core)
-    send(near.at[0:32, :], near.at[32:64, :], far_sem.at[0], {"region": after})
     for d in range(NZ):
         for k in (1, 3, 2):
             slot = slot_of(core, flip(z, d), turn(y, k))
@@ -192,102 +185,123 @@
     for zz in range(NZ):
         for yy in range(NY):
             take(slot_of(1 - core, zz, yy))
-    arrived(near.at[32:64, :], far_sem.at[0], send_sems, at)
     send.drain()
 
 
-def complex_parts(x):
-    return x[:, :QUARTER], x[:, QUARTER:HALF], x[:, HALF : HALF + QUARTER], x[:, HALF + QUARTER :]
-
-
-def spectra_of(tile_of, table):
+SEGMENTS = ((0, LANES), (QUARTER, LANES), (HALF, QUARTER))
+
+
+def spectra_of(tile_of, quarter, odd):
     pieces = [tile_of(c) for c in range(8)]
     early = jnp.concatenate(pieces[:4], axis=1)
     late = jnp.concatenate(pieces[4:], axis=1)
-    even = dot3(dot_nn, split(early + late), table[0], table[1])
-    odd = dot3(dot_nn, split(early - late), table[2], table[3])
-    return jnp.concatenate([even, odd], axis=1)
+    both = early + late
+    front, back = both[:, :QUARTER], both[:, QUARTER:]
+    return jnp.concatenate(
+        [
+            dot3(dot_nn, split(front + back), quarter[0], quarter[1]),
+            dot3(dot_nn, split(front - back), quarter[2], quarter[3]),
+            dot3(dot_nn, split(early - late), odd[0], odd[1]),
+        ],
+        axis=1,
+    )
 
 
 def cross(left, right):
-    lr, li, mr, mi = complex_parts(left)
-    rr, ri, sr, si = complex_parts(right)
-    even = jnp.concatenate([lr * rr + li * ri, li * rr - lr * ri], axis=1)
-    odd = jnp.concatenate([mr * sr + mi * si, mi * sr - mr * si], axis=1)
-    return even, odd
+    out = []
+    for base, n in SEGMENTS:
+        lr, li = left[:, base : base + n], left[:, base + n : base + 2 * n]
+        rr, ri = right[:, base : base + n], right[:, base + n : base + 2 * n]
+        out.append(jnp.concatenate([lr * rr + li * ri, li * rr - lr * ri], axis=1))
+    return out
 
 
 def halve_first(x):
-    lane = lax.broadcasted_iota(jnp.int32, (1, HALF), 1)
+    lane = lax.broadcasted_iota(jnp.int32, (1, x.shape[1]), 1)
     return x * jnp.where(lane == 0, 0.5, 1.0).astype(F32)
+
+
+def unpack(zero, two, rest, quarter, odd):
+    p0 = dot3(dot_nt, split(halve_first(zero)), quarter[0], quarter[1])
+    p2 = dot3(dot_nt, split(two), quarter[2], quarter[3])
+    return p0 + p2, p0 - p2, dot3(dot_nt, split(rest), odd[0], odd[1])
 
 
 def spread(row):
     return jnp.broadcast_to(row, (LANES, LANES)).T
 
 
+def columns(index, first):
+    rows = [spread(index[first + j : first + j + 1, :]) for j in range(TILE // LANES)]
+    return jnp.concatenate(rows, axis=0)
+
+
 def pairs_kernel(
-    count, group, near, pair_a, pair_b, observed, table, corr, remote, local, far, spec, own, conj_terms, plain_terms
+    count, group, pair_a, pair_b, observed, quarter, odd, corr, remote, local,
+    spec, full, conj_terms, plain_terms, target_lags, lags, in_sem, out_sem,
 ):
     slots = corr.shape[0]
-    spectra = spectra_of(lambda c: group[pl.ds(c, QUARTER, stride=8), :], table)
+    at = place()
+    fetch = pltpu.make_async_copy(observed, target_lags, in_sem)
+    fetch.start()
+    spectra = spectra_of(lambda c: group[pl.ds(c, QUARTER, stride=8), :], quarter, odd)
+    full[...] = spectra
     high, low = split(spectra)
     spec[0:QUARTER, :] = high
     spec[QUARTER:HALF, :] = low
-    ends = spectra_of(lambda c: near[pl.ds(c, 8, stride=8), :], table)
-    own[...] = ends
-    far_even, far_odd = cross(ends[0:4, :], ends[4:8, :])
-    far[...] = jnp.concatenate([halve_first(far_even), far_odd], axis=1)
+    mine = slot_of(at["core"], at["z"], at["y"]) * 4
+    b = pair_b[...]
+    placed = ((b >> 2) & 1) * 128 + ((b >> 3) & 7) * 16 + (b >> 6) * 4 + (b & 3)
     live_count = count[0]
     lane = lax.broadcasted_iota(jnp.int32, (TILE, LANES), 1)
-
-    def tile(i, carry):
-        rows = pl.ds(pl.multiple_of(i * TILE, TILE), TILE)
-        low_rows = pl.ds(pl.multiple_of(slots + i * TILE, TILE), TILE)
-        b_col = spread(pair_b[pl.ds(i, 1), :])
-        a_col = spread(pair_a[pl.ds(i, 1), :])
+    own = [full[pl.ds(mine + q, 1), :] for q in range(4)]
+    stores = []
+
+    for i in range(slots // TILE):
+        rows = slice(i * TILE, (i + 1) * TILE)
+        low_rows = slice(slots + i * TILE, slots + (i + 1) * TILE)
+        b_col = columns(placed, i * (TILE // LANES))
+        a_col = columns(pair_a, i * (TILE // LANES))
         hot = jnp.concatenate([b_col == lane, b_col == lane + LANES], axis=1).astype(F32).astype(BF16)
         target = dot_nn(hot, spec[0:QUARTER, :]) + dot_nn(hot, spec[QUARTER:HALF, :])
         pieces = []
         for c in range(8):
-            cut = slice(c * LANES, (c + 1) * LANES)
-            row = [jnp.broadcast_to(own[q : q + 1, cut], (TILE, LANES)) for q in range(4)]
+            row = [jnp.broadcast_to(own[q][:, c * LANES : (c + 1) * LANES], (TILE, LANES)) for q in range(4)]
             pieces.append(
                 jnp.where(a_col == 0, row[0], jnp.where(a_col == 1, row[1], jnp.where(a_col == 2, row[2], row[3])))
             )
         source = jnp.concatenate(pieces, axis=1)
-        even, odd = cross(source, target)
-        lag_even = dot3(dot_nt, split(halve_first(even)), table[0], table[1])
-        lag_odd = dot3(dot_nt, split(odd), table[2], table[3])
-        ahead = (lag_even[:, :QUARTER] + lag_odd[:, :QUARTER]) * (2.0 / WIN)
-        behind = (lag_even[:, QUARTER:] - lag_odd[:, QUARTER:]) * (2.0 / WIN)
-        number = lax.broadcasted_iota(jnp.int32, (TILE, QUARTER), 0) + i * TILE
-        live = number < live_count
-        corr[rows, 0:QUARTER] = jnp.where(live, behind, 0.0)
-        corr[rows, QUARTER:HALF] = jnp.where(live, ahead, 0.0)
-        res_behind = split(jnp.where(live, behind - observed[rows, 0:QUARTER], 0.0))
-        res_ahead = split(jnp.where(live, ahead - observed[rows, QUARTER:HALF], 0.0))
-        plus = [jnp.concatenate([res_ahead[q], res_behind[q]], axis=1) for q in (0, 1)]
-        minus = [jnp.concatenate([res_ahead[q], -res_behind[q]], axis=1) for q in (0, 1)]
-        mis_even = dot3(dot_nn, plus, table[0], table[1])
-        mis_odd = dot3(dot_nn, minus, table[2], table[3])
-        for p, mis in ((0, mis_even), (1, mis_odd)):
-            mr, mi = mis[:, :QUARTER], mis[:, QUARTER:]
-            base = p * HALF
-            sr, si = source[:, base : base + QUARTER], source[:, base + QUARTER : base + HALF]
-            tr, ti = target[:, base : base + QUARTER], target[:, base + QUARTER : base + HALF]
+        front, back, rest = unpack(*cross(source, target), quarter, odd)
+        ahead = (front + rest[:, :QUARTER]) * (2.0 / WIN)
+        behind = (back - rest[:, QUARTER:]) * (2.0 / WIN)
+        live = lax.broadcasted_iota(jnp.int32, (TILE, QUARTER), 0) + i * TILE < live_count
+        lags[rows, 0:QUARTER] = jnp.where(live, behind, 0.0)
+        lags[rows, QUARTER:HALF] = jnp.where(live, ahead, 0.0)
+        if i == 0:
+            fetch.wait()
+        res_behind = jnp.where(live, behind - target_lags[rows, 0:QUARTER], 0.0)
+        res_ahead = jnp.where(live, ahead - target_lags[rows, QUARTER:HALF], 0.0)
+        store = pltpu.make_async_copy(lags.at[rows, :], corr.at[rows, :], out_sem.at[i])
+        store.start()
+        stores.append(store)
+        misfit = (
+            dot3(dot_nn, split(res_ahead + res_behind), quarter[0], quarter[1]),
+            dot3(dot_nn, split(res_ahead - res_behind), quarter[2], quarter[3]),
+            dot3(dot_nn, split(jnp.concatenate([res_ahead, -res_behind], axis=1)), odd[0], odd[1]),
+        )
+        for (base, n), mis in zip(SEGMENTS, misfit):
+            mr, mi = mis[:, :n], mis[:, n:]
+            sr, si = source[:, base : base + n], source[:, base + n : base + 2 * n]
+            tr, ti = target[:, base : base + n], target[:, base + n : base + 2 * n]
             for terms, re, im in (
                 (conj_terms, mr * sr + mi * si, mr * si - mi * sr),
                 (plain_terms, mr * tr - mi * ti, mr * ti + mi * tr),
             ):
-                for offset, part in ((0, re), (QUARTER, im)):
+                for offset, part in ((0, re), (n, im)):
                     part_high, part_low = split(part)
-                    cut = slice(base + offset, base + offset + QUARTER)
+                    cut = slice(base + offset, base + offset + n)
                     terms[rows, cut] = part_high
                     terms[low_rows, cut] = part_low
-        return carry
-
-    lax.fori_loop(0, slots // TILE, tile, 0)
 
     def hot_rows(index, height):
         down = lax.broadcasted_iota(jnp.int32, (height, LANES), 0)
@@ -297,21 +311,35 @@
         ]
         return jnp.concatenate(cols + cols, axis=1)
 
-    totals = dot_nn(hot_rows(pair_b, QUARTER), conj_terms[...])
+    totals = dot_nn(hot_rows(placed, QUARTER), conj_terms[...])
     own_totals = dot_nn(hot_rows(pair_a, 8), plain_terms[...])
     for c in range(8):
         remote[pl.ds(c, QUARTER, stride=8), :] = totals[:, c * LANES : (c + 1) * LANES]
     local[...] = own_totals
+    for store in stores:
+        store.wait()
 
 
 def reduce_kernel(
-    remote, local, far, table, adjoint, far_corr, plane_in, ring_in, mate_in, sums, total,
-    send_sems, plane_sems, ring_sems, mate_sems,
+    remote, local, near, quarter_hbm, odd_hbm, adjoint, far_corr, plane_in, ring_in, mate_in, sums, total, ends,
+    quarter, odd, send_sems, plane_sems, ring_sems, mate_sems, far_sem, table_sems,
 ):
     at = place()
     y, z, core = at["y"], at["z"], at["core"]
+    region = lax.axis_index("region")
+    regions = lax.axis_size("region")
+    after, before = lax.rem(region + 1, regions), lax.rem(region + regions - 1, regions)
     barrier, count = enter(at)
-    pl.semaphore_wait(barrier, count)
+    for other in (after, before):
+        pl.semaphore_signal(barrier, inc=1, device_id={"region": other}, device_id_type=MESH)
+    fetches = [
+        pltpu.make_async_copy(quarter_hbm, quarter, table_sems.at[0]),
+        pltpu.make_async_copy(odd_hbm, odd, table_sems.at[1]),
+    ]
+    for fetch in fetches:
+        fetch.start()
+    ends[0:32, :] = near[...]
+    pl.semaphore_wait(barrier, count + 2)
     send = Sender(send_sems)
     outward = (7, 6, 5, 4, 3, 2, 1, 0)
 
@@ -335,6 +363,7 @@
             plane_sems.at[d],
             {"blk": device(y, z, 1 - core)},
         )
+    send(near, ends.at[32:64, :], far_sem.at[0], {"region": after})
     for d in outward:
         zz = flip(z, d)
         arrived(plane_in.at[part(0, zz), :], plane_sems.at[d], send_sems, at)
@@ -356,6 +385,11 @@
             send(
                 total.at[mate(d), :], mate_in.at[mate(d), :], mate_sems.at[d], {"blk": device(y, flip(z, d), core)}
             )
+    for fetch in fetches:
+        fetch.wait()
+    arrived(ends.at[32:64, :], far_sem.at[0], send_sems, at)
+    spectra = spectra_of(lambda c: ends[pl.ds(c, 8, stride=8), :], quarter, odd)
+    far = cross(spectra[0:4, :], spectra[4:8, :])
     summed = total[mate(0), :]
     for d in (1, 2, 3, 4, 5, 6, 7):
         arrived(mate_in.at[mate(d), :], mate_sems.at[d], send_sems, at)
@@ -364,12 +398,16 @@
 
     pieces = [total[pl.ds(c, 4, stride=8), :] for c in range(8)]
     source = jnp.concatenate(pieces, axis=1) + local[0:4, :]
-    even = jnp.concatenate([halve_first(source[:, :HALF]), far[:, :HALF]], axis=0)
-    odd = jnp.concatenate([source[:, HALF:], far[:, HALF:]], axis=0)
-    lag_even = dot3(dot_nt, split(even), table[0], table[1])
-    lag_odd = dot3(dot_nt, split(odd), table[2], table[3])
-    plus = (lag_even + lag_odd) * (2.0 / WIN)
-    minus = (lag_even - lag_odd) * (2.0 / WIN)
+    front, back, rest = unpack(
+        *[
+            jnp.concatenate([source[:, base : base + 2 * n], far[i]], axis=0)
+            for i, (base, n) in enumerate(SEGMENTS)
+        ],
+        quarter,
+        odd,
+    )
+    plus = (jnp.concatenate([front, back], axis=1) + rest) * (2.0 / WIN)
+    minus = (jnp.concatenate([front, back], axis=1) - rest) * (2.0 / WIN)
     adjoint[:, :HALF] = plus[0:4, :] * (1.0 / 16.0)
     adjoint[:, HALF:] = minus[0:4, :] * (1.0 / 16.0)
     far_corr[:, :QUARTER] = minus[4:8, QUARTER:]
@@ -385,6 +423,10 @@
     return pl.BlockSpec(memory_space=pltpu.SMEM)
 
 
+def anywhere():
+    return pl.BlockSpec(memory_space=pl.ANY)
+
+
 def params(**kw):
     return pltpu.CompilerParams(vmem_limit_bytes=56 * 1024 * 1024, **kw)
 
@@ -392,53 +434,54 @@
 def body(records, starts, tapers, pair_a, pair_b, pair_count, observed):
     slots = pair_a.shape[0]
     shape = jax.ShapeDtypeStruct
-    table = jnp.asarray(tables())
+    quarter, odd = (jnp.asarray(table) for table in tables())
     group, near = pl.pallas_call(
         gather_kernel,
-        out_shape=(shape((2048, LANES), F32), shape((64, LANES), F32)),
+        out_shape=(shape((2048, LANES), F32), shape((32, LANES), F32)),
         in_specs=[smem(), smem(), vmem()],
         out_specs=(vmem(), vmem()),
         scratch_shapes=[
             pltpu.VMEM((64, LANES), F32),
             pltpu.SemaphoreType.DMA((72,)),
             pltpu.SemaphoreType.DMA((64,)),
-            pltpu.SemaphoreType.DMA((1,)),
         ],
         compiler_params=params(collective_id=0, has_side_effects=True),
         name="gather_windows",
     )(starts, tapers, records)
-    placed = (pair_b // 4 % 2) * 128 + (pair_b // 8 % NZ) * 16 + (pair_b // 64) * 4 + pair_b % 4
-    corr, remote, local, far = pl.pallas_call(
+    corr, remote, local = pl.pallas_call(
         pairs_kernel,
         out_shape=(
             shape((slots, HALF), F32),
             shape((2048, LANES), F32),
             shape((8, WIN), F32),
-            shape((4, WIN), F32),
         ),
-        in_specs=[smem()] + [vmem()] * 6,
-        out_specs=(vmem(),) * 4,
+        in_specs=[smem()] + [vmem()] * 3 + [anywhere()] + [vmem()] * 2,
+        out_specs=(anywhere(), vmem(), vmem()),
         scratch_shapes=[
             pltpu.VMEM((HALF, WIN), BF16),
-            pltpu.VMEM((8, WIN), F32),
+            pltpu.VMEM((QUARTER, WIN), F32),
             pltpu.VMEM((2 * slots, WIN), BF16),
             pltpu.VMEM((2 * slots, WIN), BF16),
+            pltpu.VMEM((slots, HALF), F32),
+            pltpu.VMEM((slots, HALF), F32),
+            pltpu.SemaphoreType.DMA,
+            pltpu.SemaphoreType.DMA((slots // TILE,)),
         ],
         compiler_params=params(),
         name="pairs",
     )(
         pair_count,
         group,
-        near,
         pair_a.reshape(slots // LANES, LANES),
-        placed.reshape(slots // LANES, LANES),
+        pair_b.reshape(slots // LANES, LANES),
         observed,
-        table,
+        quarter,
+        odd,
     )
     adjoint, far_corr = pl.pallas_call(
         reduce_kernel,
         out_shape=(shape((4, WIN), F32), shape((4, HALF), F32)),
-        in_specs=[vmem()] * 4,
+        in_specs=[vmem()] * 3 + [anywhere()] * 2,
         out_specs=(vmem(), vmem()),
         scratch_shapes=[
             pltpu.VMEM((1024, LANES), F32),
@@ -446,14 +489,19 @@
             pltpu.VMEM((256, LANES), F32),
             pltpu.VMEM((1024, LANES), F32),
             pltpu.VMEM((256, LANES), F32),
+            pltpu.VMEM((64, LANES), F32),
+            pltpu.VMEM(quarter.shape, BF16),
+            pltpu.VMEM(odd.shape, BF16),
             pltpu.SemaphoreType.DMA((40,)),
             pltpu.SemaphoreType.DMA((8,)),
             pltpu.SemaphoreType.DMA((24,)),
             pltpu.SemaphoreType.DMA((8,)),
+            pltpu.SemaphoreType.DMA((1,)),
+            pltpu.SemaphoreType.DMA((2,)),
         ],
         compiler_params=params(collective_id=1, has_side_effects=True),
         name="reduce_terms",
-    )(remote, local, far, table)
+    )(remote, local, near, quarter, odd)
     return corr, far_corr, adjoint
 
 

time: 82.2 us -> 72.3 us (0.88)
  Pallas kernels: 76.6 us -> 68 us
  other arithmetic: 1.3 us -> 0 us
    pallas_call x1, Pallas kernels: 19.1 us -> 12.1 us  [body(): pl.pallas_call(pairs_kernel, out_shape=(shape((slots, HALF), F32), shape(...]
    pallas_call x1, Pallas kernels: 36.5 us -> 30.6 us  [body(): pl.pallas_call(gather_kernel, out_shape=(shape((2048, LANES), F32), shape...]
    pallas_call x1, Pallas kernels: 21 us -> 25.3 us  [body(): pl.pallas_call(reduce_kernel, out_shape=(shape((4, WIN), F32), shape((4,...]
    reshape x1 -> x0, other arithmetic: 1.3 us -> none  [body(): placed.reshape(slots // LANES, LANES)]
where the time goes in v3:
time: 72.3 us; the launch traced here: 71.9 us
  Pallas kernels  68 us (94%)
  local copies, waits for them, and re-layouts  2.62 us (4%)
  between operations  1.3 us (2%)
    pallas_call x1, Pallas kernels, body(): pl.pallas_call(gather_kernel, out_shape=(shape((2048, LANES), F32), shape...  30.6 us
    pallas_call x1, Pallas kernels, body(): pl.pallas_call(reduce_kernel, out_shape=(shape((4, WIN), F32), shape((4,...  25.3 us
    pallas_call x1, Pallas kernels, body(): pl.pallas_call(pairs_kernel, out_shape=(shape((slots, HALF), F32), shape(...  12.1 us
    unnamed x2, local copies, waits for them, and re-layouts  2.62 us

profile of v3, /device:TPU:1, one launch (start us, length us, event | category | flops | bytes accessed | tf_op | source)
XLA Modules:
  0.0 71.9 jit_solution(11720223341165627404)
XLA Ops:
  1.3 30.6 %gather_windows.1 = (f32[2048,128]{1,0:T(8,128)}, f32[32,128]{1,0:T(8,128)}) custom-call(s32[4]{0:T(128)} %starts.1, s32[4]{0:T(128)} %tapers.1, f32[4,2048]{1,0:T(4,128)} %records.1), custom_call_target="tpu_custom_call" | custom-call | tf_op jit(solution)/shard_map/gather_windows/pallas_call | solution.py:438
  31.9 12.1 %pairs.1 = (f32[768,512]{1,0:T(8,128)}, f32[2048,128]{1,0:T(8,128)}, f32[8,1024]{1,0:T(8,128)}) custom-call(s32[1]{0:T(128)S(6)} %copy.14.count, f32[2048,128]{1,0:T(8,128)} %get-tuple-element.10.group, s32[6,128]{1,0:T(8,128)} %bitcast.2, s32[6,128]{1,0:T(8,128)} %bitcast.3, f32[768,512]{1,0:T(8,128)} %observed.1, ...), custom_call_target="tpu_custom_call" | custom-call | tf_op jit(solution)/shard_map/pairs/pallas_call | solution.py:451
  44.0 25.3 %reduce_terms.1 = (f32[4,1024]{1,0:T(4,128)}, f32[4,512]{1,0:T(4,128)}) custom-call(f32[2048,128]{1,0:T(8,128)} %get-tuple-element.12.remote, f32[8,1024]{1,0:T(8,128)} %get-tuple-element.13.local, f32[32,128]{1,0:T(8,128)} %get-tuple-element.14.near, bf16[4,256,256]{2,1,0:T(8,128)(2,1)} %constant.4.clone.quarter.quarter_hbm, ...), custom_call_target="tpu_custom_call" | custom-call | tf_op jit(solution)/shard_map/reduce_terms/pallas_call | solution.py:481
  69.3 1.3 %copy.15 = f32[4,512]{1,0:T(4,128)} copy(f32[4,512]{1,0:T(4,128)} %get-tuple-element.21) | data formatting | bytes 16384
  70.6 1.3 %copy.16 = f32[4,1024]{1,0:T(4,128)} copy(f32[4,1024]{1,0:T(4,128)} %get-tuple-element.22) | data formatting | bytes 32768

commit v4 on v3

--- a/solution.py
+++ b/solution.py
@@ -252,7 +252,7 @@
     mine = slot_of(at["core"], at["z"], at["y"]) * 4
     b = pair_b[...]
     placed = ((b >> 2) & 1) * 128 + ((b >> 3) & 7) * 16 + (b >> 6) * 4 + (b & 3)
-    live_count = count[0]
+    live_count = count[...]
     lane = lax.broadcasted_iota(jnp.int32, (TILE, LANES), 1)
     own = [full[pl.ds(mine + q, 1), :] for q in range(4)]
     stores = []
@@ -321,7 +321,7 @@
 
 
 def reduce_kernel(
-    remote, local, near, quarter_hbm, odd_hbm, adjoint, far_corr, plane_in, ring_in, mate_in, sums, total, ends,
+    remote, local, near, quarter_hbm, odd_hbm, lines, plane_in, ring_in, mate_in, sums, total, ends,
     quarter, odd, send_sems, plane_sems, ring_sems, mate_sems, far_sem, table_sems,
 ):
     at = place()
@@ -330,8 +330,7 @@
     regions = lax.axis_size("region")
     after, before = lax.rem(region + 1, regions), lax.rem(region + regions - 1, regions)
     barrier, count = enter(at)
-    for other in (after, before):
-        pl.semaphore_signal(barrier, inc=1, device_id={"region": other}, device_id_type=MESH)
+    pl.semaphore_signal(barrier, inc=1, device_id={"region": before}, device_id_type=MESH)
     fetches = [
         pltpu.make_async_copy(quarter_hbm, quarter, table_sems.at[0]),
         pltpu.make_async_copy(odd_hbm, odd, table_sems.at[1]),
@@ -339,7 +338,7 @@
     for fetch in fetches:
         fetch.start()
     ends[0:32, :] = near[...]
-    pl.semaphore_wait(barrier, count + 2)
+    pl.semaphore_wait(barrier, count + 1)
     send = Sender(send_sems)
     outward = (7, 6, 5, 4, 3, 2, 1, 0)
 
@@ -408,11 +407,15 @@
     )
     plus = (jnp.concatenate([front, back], axis=1) + rest) * (2.0 / WIN)
     minus = (jnp.concatenate([front, back], axis=1) - rest) * (2.0 / WIN)
-    adjoint[:, :HALF] = plus[0:4, :] * (1.0 / 16.0)
-    adjoint[:, HALF:] = minus[0:4, :] * (1.0 / 16.0)
-    far_corr[:, :QUARTER] = minus[4:8, QUARTER:]
-    far_corr[:, QUARTER:] = plus[4:8, :QUARTER]
+    lines[:, :HALF] = plus
+    lines[:, HALF:] = minus
     send.drain()
+
+
+def place_kernel(lines, adjoint, far_corr):
+    adjoint[...] = lines[0:4, :] * (1.0 / 16.0)
+    far_corr[:, :QUARTER] = lines[4:8, WIN - QUARTER :]
+    far_corr[:, QUARTER:] = lines[4:8, :QUARTER]
 
 
 def vmem():
@@ -455,7 +458,7 @@
             shape((2048, LANES), F32),
             shape((8, WIN), F32),
         ),
-        in_specs=[smem()] + [vmem()] * 3 + [anywhere()] + [vmem()] * 2,
+        in_specs=[vmem()] * 4 + [anywhere()] + [vmem()] * 2,
         out_specs=(anywhere(), vmem(), vmem()),
         scratch_shapes=[
             pltpu.VMEM((HALF, WIN), BF16),
@@ -470,7 +473,7 @@
         compiler_params=params(),
         name="pairs",
     )(
-        pair_count,
+        pair_count.reshape(1, 1),
         group,
         pair_a.reshape(slots // LANES, LANES),
         pair_b.reshape(slots // LANES, LANES),
@@ -478,11 +481,11 @@
         quarter,
         odd,
     )
-    adjoint, far_corr = pl.pallas_call(
+    lines = pl.pallas_call(
         reduce_kernel,
-        out_shape=(shape((4, WIN), F32), shape((4, HALF), F32)),
+        out_shape=shape((8, WIN), F32),
         in_specs=[vmem()] * 3 + [anywhere()] * 2,
-        out_specs=(vmem(), vmem()),
+        out_specs=vmem(),
         scratch_shapes=[
             pltpu.VMEM((1024, LANES), F32),
             pltpu.VMEM((768, LANES), F32),
@@ -502,6 +505,14 @@
         compiler_params=params(collective_id=1, has_side_effects=True),
         name="reduce_terms",
     )(remote, local, near, quarter, odd)
+    adjoint, far_corr = pl.pallas_call(
+        place_kernel,
+        out_shape=(shape((4, WIN), F32), shape((4, HALF), F32)),
+        in_specs=[vmem()],
+        out_specs=(vmem(), vmem()),
+        compiler_params=params(),
+        name="place_lines",
+    )(lines)
     return corr, far_corr, adjoint
 
 

time: 72.3 us -> 67.2 us (0.929)
  the two profiles are of different devices: /device:TPU:1 before, /device:TPU:6 now
where the time goes in v4:
time: 67.2 us; the launch traced here: 66.8 us
  Pallas kernels  65.5 us (97%)
  between operations  1.3 us (2%)
    pallas_call x1, Pallas kernels, body(): pl.pallas_call(gather_kernel, out_shape=(shape((2048, LANES), F32), shape...  29.2 us
    pallas_call x1, Pallas kernels, body(): pl.pallas_call(reduce_kernel, out_shape=shape((8, WIN), F32), in_specs=[v...  23.9 us
    pallas_call x1, Pallas kernels, body(): pl.pallas_call(pairs_kernel, out_shape=(shape((slots, HALF), F32), shape(...  11.1 us
    pallas_call x1, Pallas kernels, body(): pl.pallas_call(place_kernel, out_shape=(shape((4, WIN), F32), shape((4, H...  1.37 us

profile of v4, /device:TPU:6, one launch (start us, length us, event | category | flops | bytes accessed | tf_op | source)
XLA Modules:
  0.0 66.8 jit_solution(4212176572723735322)
XLA Ops:
  1.3 29.2 %gather_windows.1 = (f32[2048,128]{1,0:T(8,128)}, f32[32,128]{1,0:T(8,128)}) custom-call(s32[4]{0:T(128)} %starts.1, s32[4]{0:T(128)} %tapers.1, f32[4,2048]{1,0:T(4,128)} %records.1), custom_call_target="tpu_custom_call" | custom-call | tf_op jit(solution)/shard_map/gather_windows/pallas_call | solution.py:441
  30.5 11.1 %pairs.1 = (f32[768,512]{1,0:T(8,128)}, f32[2048,128]{1,0:T(8,128)}, f32[8,1024]{1,0:T(8,128)}) custom-call(s32[1,1]{1,0:T(1,128)} %bitcast.3.count, f32[2048,128]{1,0:T(8,128)} %get-tuple-element.10.group, s32[6,128]{1,0:T(8,128)} %bitcast.4, s32[6,128]{1,0:T(8,128)} %bitcast.5, f32[768,512]{1,0:T(8,128)} %observed.1, ...), custom_call_target="tpu_custom_call" | custom-call | tf_op jit(solution)/shard_map/pairs/pallas_call | solution.py:454
  41.6 23.9 %reduce_terms.1.lines = f32[8,1024]{1,0:T(8,128)} custom-call(f32[2048,128]{1,0:T(8,128)} %get-tuple-element.12.remote, f32[8,1024]{1,0:T(8,128)} %get-tuple-element.13.local, f32[32,128]{1,0:T(8,128)} %get-tuple-element.14.near, bf16[4,256,256]{2,1,0:T(8,128)(2,1)} %constant.4.clone.quarter.quarter_hbm, bf16[2,512,512]{2,1,0:T(8,128)(2,1)} %constant.5.clone.odd.odd_hbm), custom_call_target="tpu_custom_call" | custom-call | tf_op jit(solution)/shard_map/reduce_terms/pallas_call | solution.py:484
  65.5 1.4 %place_lines.1 = (f32[4,1024]{1,0:T(4,128)}, f32[4,512]{1,0:T(4,128)}) custom-call(f32[8,1024]{1,0:T(8,128)} %reduce_terms.1.lines), custom_call_target="tpu_custom_call" | custom-call | tf_op jit(solution)/shard_map/place_lines/pallas_call | solution.py:508
